TPU v7x, 512 devices: a whole 4x4x16 slice. The times are simulated.
512 devices in a mesh: prow: 16 (over y_hi, x, core), pcol: 32 (over y_lo, z).
Axes of the slice: x: 4, y: 4 (y_hi: 2, y_lo: 2; y = y_hi * 2 + y_lo), z: 16, core: 2. Of those that a mesh axis runs over, the one named last changes fastest.
Arguments:
- sep_inverse: bfloat16 [2, 16, 256, 1, 32, 256], P(None, 'prow', None, None, 'pcol'), may hold values from -2 to 30, as said below
- panels: bfloat16 [4, 2, 16, 256, 256], P(None, None, 'prow', 'pcol'), may hold values from -0.0625 to 0.0625
- ancestors: int32 [4, 32], replicated, may hold values from 0 to 1, as said below
- window_factor: bfloat16 [6, 256, 256], replicated, may hold values from -0.1875 to 0.1875
- diag_inverse: bfloat16 [4, 256, 256], replicated, may hold values from -1 to 4, as said below
Outputs:
- ys: float32 [4, 2, 16, 256, 256], P(None, None, 'prow', 'pcol')
- window_inverse: float32 [1024, 1024], P('prow', 'pcol')
Inputs may be any that keep to these rules, and one draw needn't show every extreme that they name: sep_inverse read as in the first step is symmetric. `diag_inverse`: each block is symmetric. ancestors[k + 1, t] <= ancestors[k, t]: a supernode's ancestor tiles lie among those of the one before it.
All inputs are finite; a program needn't handle non-finite values.
Results may differ from a plain program's by a relative error of at most 0.00035.
Values may be sent and summed in bfloat16 or wider, within the bound.
A program may use at most 64 MiB of HBM per device.

v0:
```python
import jax
import jax.numpy as jnp
from jax import lax
from jax.sharding import PartitionSpec as P


def broadcast(block, axis, owner):
    block = jnp.where(lax.axis_index(axis) == owner, block, jnp.zeros_like(block))
    return lax.psum(block, axis)


def product(operand_left, operand_right):
    return jnp.dot(
        operand_left,
        operand_right,
        precision=lax.Precision.HIGHEST,
        preferred_element_type=jnp.float32,
    )


def pair_index(earlier, later):
    return later * (later - 1) // 2 + earlier


def window_step(later, window_sums, window_factor, diag_inverse, window_blocks):
    coupled = []
    for earlier in range(later):
        running = window_sums[earlier]
        for partner in range(later):
            running = running + product(
                window_blocks[earlier, partner],
                window_factor[pair_index(partner, later)].astype(jnp.float32),
            )
        upper_block = -running
        window_blocks[earlier, later] = upper_block
        window_blocks[later, earlier] = upper_block.T
        coupled.append(upper_block)
    running = window_sums[later]
    for earlier in range(later):
        running = running + product(
            window_factor[pair_index(earlier, later)].astype(jnp.float32).T, coupled[earlier]
        )
    window_blocks[later, later] = diag_inverse[later].astype(jnp.float32) - running


def assemble_window(window_blocks, supernodes):
    return jnp.block(
        [
            [window_blocks[first, second] for second in range(supernodes)]
            for first in range(supernodes)
        ]
    )


def per_device(sep_inverse, panels, ancestors, window_factor, diag_inverse):
    prow_count = lax.axis_size("prow")
    pcol_count = lax.axis_size("pcol")
    row_index = lax.axis_index("prow")
    column_index = lax.axis_index("pcol")
    tile_rows = sep_inverse.shape[0]
    width = sep_inverse.shape[2]
    owned_count = sep_inverse.shape[3]
    supernodes = panels.shape[0]
    slice_rows = panels.shape[3]
    group_ratio = pcol_count // prow_count
    local_sep = sep_inverse.reshape(tile_rows, width, owned_count, width)
    window_blocks = {}
    columns = []
    for later in range(supernodes):
        tile_flags = lax.dynamic_slice_in_dim(
            ancestors[later].reshape(tile_rows, prow_count), row_index, 1, 1
        )
        keep_tiles = tile_flags.astype(jnp.bfloat16).reshape(tile_rows, 1, 1)
        own_piece = panels[later, :, 0] * keep_tiles
        full_rows = lax.all_gather(own_piece, "pcol", axis=1, tiled=True)
        grouped = full_rows.reshape(owned_count, group_ratio, width, width)
        picked = lax.dynamic_slice_in_dim(grouped, column_index // prow_count, 1, 1)[:, 0]
        owned_tiles = broadcast(picked, "prow", column_index % prow_count)

        def row_term(first_row, row_count, owned_tiles=owned_tiles):
            return jnp.einsum(
                "rbcd,cde->bre", local_sep, owned_tiles, preferred_element_type=jnp.float32
            )

        summed = lax.psum_scatter(
            row_term(jnp.int32(0), slice_rows * lax.axis_size("pcol")),
            "pcol",
            scatter_dimension=0,
            tiled=True,
        )
        row_total = jnp.transpose(summed, (1, 0, 2)).reshape(tile_rows * slice_rows, width)
        row_keep = jnp.repeat(
            tile_flags[:, 0].astype(jnp.float32),
            slice_rows,
            total_repeat_length=tile_rows * slice_rows,
        )
        carried = -row_total
        for earlier in range(later):
            carried = carried - product(
                columns[earlier], window_factor[pair_index(earlier, later)].astype(jnp.float32)
            )
        current = carried * row_keep[:, None]
        factor_rows = own_piece.reshape(tile_rows * slice_rows, width).astype(jnp.float32)
        window_parts = [product(columns[earlier].T, factor_rows) for earlier in range(later)]
        window_parts.append(product(factor_rows.T, current))
        window_sums = lax.psum(jnp.stack(window_parts), ("prow", "pcol"))
        window_step(later, window_sums, window_factor, diag_inverse, window_blocks)
        columns.append(current)
    ys = jnp.stack(columns).reshape(supernodes, tile_rows, 1, slice_rows, width)
    whole_window = assemble_window(window_blocks, supernodes)
    rows_each = supernodes * width // prow_count
    cols_each = supernodes * width // pcol_count
    local_window = lax.dynamic_slice(
        whole_window, (row_index * rows_each, column_index * cols_each), (rows_each, cols_each)
    )
    return (ys, local_window)


def solution(mesh):
    placed = (
        P(None, "prow", None, None, "pcol", None),
        P(None, None, "prow", "pcol", None),
        P(),
        P(),
        P(),
    )
    return jax.shard_map(
        per_device,
        mesh=mesh,
        in_specs=placed,
        out_specs=(P(None, None, "prow", "pcol", None), P("prow", "pcol")),
        check_vma=False,
    )
```

profile of v0, /device:TPU:4, one launch (start us, length us, event | category | flops | bytes accessed | tf_op | source)
XLA Modules:
  0.0 1206.1 jit_solution(4849116906709062268)
XLA Ops:
  7.3 0.8 slice_reduce_fusion.1
  8.9 0.8 bitcast_multiply_fusion.6
  9.8 70.2 %all_gather.12 = bf16[2,256,256]{2,0,1:T(2,128)(2,1)S(1)} all-gather(bf16[2,8,256]{2,0,1:T(2,128)(2,1)S(1)} %copy.58), channel_id=1, replica_groups=mesh['prow'=16,'pcol'=32] {'pcol'}, dimensions={1}, use_global_device_ids=true | all-gather | bytes 270336 | tf_op jit(solution)/shard_map/all_gather | solution.py:75
  80.4 59.8 %all_gather.13 = bf16[2,256,256]{2,0,1:T(2,128)(2,1)S(1)} all-gather(bf16[2,8,256]{2,0,1:T(2,128)(2,1)S(1)} %copy.63), channel_id=1, replica_groups=mesh['prow'=16,'pcol'=32] {'pcol'}, dimensions={1}, use_global_device_ids=true | all-gather | bytes 270336 | tf_op jit(solution)/shard_map/all_gather | solution.py:75
  142.0 61.7 %all_gather.15 = bf16[2,256,256]{2,0,1:T(2,128)(2,1)S(1)} all-gather(bf16[2,8,256]{2,0,1:T(2,128)(2,1)S(1)} %copy.73), channel_id=1, replica_groups=mesh['prow'=16,'pcol'=32] {'pcol'}, dimensions={1}, use_global_device_ids=true | all-gather | bytes 270336 | tf_op jit(solution)/shard_map/all_gather | solution.py:75
  204.8 59.8 %all_gather.14 = bf16[2,256,256]{2,0,1:T(2,128)(2,1)S(1)} all-gather(bf16[2,8,256]{2,0,1:T(2,128)(2,1)S(1)} %copy.68), channel_id=1, replica_groups=mesh['prow'=16,'pcol'=32] {'pcol'}, dimensions={1}, use_global_device_ids=true | all-gather | bytes 270336 | tf_op jit(solution)/shard_map/all_gather | solution.py:75
  265.8 141.1 %all-reduce.15.cloned.1.call-done = (bf16[256,256]{0,1:T(8,128)(2,1)}, bf16[256,256]{0,1:T(8,128)(2,1)}, bf16[256,256]{0,1:T(8,128)(2,1)}, bf16[256,256]{0,1:T(8,128)(2,1)}) async-done(((bf16[256,256]{0,1:T(8,128)(2,1)}, bf16[256,256]{0,1:T(8,128)(2,1)}, bf16[256,256]{0,1:T(8,128)(2,1)}, bf16[256,256]{0,1:T(8,128)(2,1)}), (bf16[256,256]{0,1:T(8,128)(2,1)}, bf16[256,256]{0,1:T(8,128)(2,1)}, ...) | async-done | bytes 524304 | tf_op jit(solution)/shard_map/psum | solution.py:9
  406.9 1.2 convolution_bitcast_fusion
  408.1 1.0 copy.75
  409.3 1.0 copy.60
  410.6 1.0 copy.65
  411.9 1.0 copy.70
  416.5 5.0 broadcast_select_fusion
  421.6 1.3 dynamic-slice.31
  423.5 262.1 %all-reduce.13.cloned.1.call-done = (f32[256,2,256]{2,1,0:T(2,128)}, f32[256,2,256]{2,1,0:T(2,128)}, f32[256,2,256]{2,1,0:T(2,128)}, f32[256,2,256]{2,1,0:T(2,128)}) async-done(((f32[256,2,256]{2,1,0:T(2,128)}, f32[256,2,256]{2,1,0:T(2,128)}, f32[256,2,256]{2,1,0:T(2,128)}, f32[256,2,256]{2,1,0:T(2,128)}), (f32[256,2,256]{2,1,0:T(2,128)}, f32[256,2,256]{2,1,0:T(2,128)}, f32[256,2,256]{2,1,0:T(2,128)}, ...) | async-done | bytes 2097168
  687.6 1.1 convolution_bitcast_fusion.19
  694.2 0.8 pad_maximum_fusion.2
  695.0 0.9 pad_maximum_fusion.1
  696.0 1.1 pad_maximum_fusion
  697.8 481.1 %all-reduce.11.cloned.1.call-done = (f32[1,256,256]{2,1,0:T(8,128)}, f32[4,256,256]{2,1,0:T(8,128)}, f32[2,256,256]{2,1,0:T(8,128)}, f32[3,256,256]{2,1,0:T(8,128)}) async-done(((f32[1,256,256]{2,1,0:T(8,128)}, f32[4,256,256]{2,1,0:T(8,128)}, f32[2,256,256]{2,1,0:T(8,128)}, f32[3,256,256]{2,1,0:T(8,128)}), (f32[1,256,256]{2,1,0:T(8,128)}, f32[4,256,256]{2,1,0:T(8,128)}, f32[2,256,256]{2,1,0:T(8,128)}, ...) | async-done | bytes 2621456 | tf_op jit(solution)/shard_map/psum | solution.py:106
  1178.9 1.0 subtract_bitcast_fusion
  1179.9 1.3 fusion.14
  1183.6 1.0 fusion.7
  1185.1 0.8 copy.82
  1186.7 0.9 copy.86
  1187.6 0.9 copy.91
  1189.4 1.2 fusion.6
  1190.6 0.8 copy.85
  1191.4 2.0 fusion.3
  1193.4 0.8 copy.90
  1195.8 1.9 fusion.1
  1197.9 1.1 maximum_maximum_fusion
  (108 shorter events, 24.6 us)
Async XLA Ops:
  7.2 399.7 %copy-start = (bf16[2,1,256,1,1,256]{5,2,4,3,1,0:T(8,128)(2,1)S(1)}, bf16[2,1,256,1,1,256]{5,2,4,3,1,0:T(8,128)(2,1)}, u32[]{:S(2)}) copy-start(bf16[2,1,256,1,1,256]{5,2,4,3,1,0:T(8,128)(2,1)} %param.15) | copy-start | bytes 786436
  7.2 399.7 %all-reduce.15.cloned.1.call-start = ((), (), s32[]{:S(2)}) async-start(), calls=%async_computation.2 | async-start | bytes 1048576 | tf_op jit(solution)/shard_map/psum | solution.py:9
  265.7 420.0 %all-reduce.13.cloned.1.call-start = ((), (), s32[]{:S(2)}) async-start(), calls=%async_computation.1 | async-start | bytes 4194304
  406.9 2.2 copy-start.11
  409.1 1.3 copy-start.10
  410.3 1.3 copy-start.9
  412.9 3.6 copy-start.12
  412.9 273.5 %copy-start.8 = (bf16[4,2,1,8,256]{4,3,2,1,0:T(8,128)(2,1)S(1)}, bf16[4,2,1,8,256]{4,3,2,1,0:T(8,128)(2,1)}, u32[]{:S(2)}) copy-start(bf16[4,2,1,8,256]{4,3,2,1,0:T(8,128)(2,1)} %param.16) | copy-start | bytes 98308
  412.9 277.2 %copy-start.1 = (bf16[6,256,256]{2,1,0:T(8,128)(2,1)S(1)}, bf16[6,256,256]{2,1,0:T(8,128)(2,1)}, u32[]{:S(2)}) copy-start(bf16[6,256,256]{2,1,0:T(8,128)(2,1)} %param.18) | copy-start | bytes 2359300
  412.9 765.9 %all-reduce.11.cloned.1.call-start = ((), (), s32[]{:S(2)}) async-start(), calls=%async_computation | async-start | bytes 5242880 | tf_op jit(solution)/shard_map/psum | solution.py:106
  697.1 481.8 %copy-start.7 = (bf16[4,256,256]{2,1,0:T(8,128)(2,1)S(1)}, bf16[4,256,256]{2,1,0:T(8,128)(2,1)}, u32[]{:S(2)}) copy-start(bf16[4,256,256]{2,1,0:T(8,128)(2,1)} %param.19) | copy-start | bytes 1572868
  1178.9 2.4 copy-start.6
  1179.9 1.7 copy-start.2
  1181.6 1.1 copy-start.5
  1188.4 0.9 copy-start.4
  1194.3 0.9 copy-start.3
Sparse Core Ops, SparseCore 0:
  265.8 140.9 all-reduce.14
  413.1 272.5 all-reduce.12
  697.2 481.5 all-reduce.10
where the time goes:
time: 1210 us
  waiting for transfers between devices  884 us (73%)
  blocking collectives  252 us (21%)
  local copies, waits for them, and re-layouts  20.5 us (2%)
  matrix products  19.6 us (2%)
  other arithmetic  15 us (1%)
  between operations  14.9 us (1%)
    psum x1, waiting for transfers between devices, per_device(): window_sums = lax.psum(jnp.stack(window_parts), ('prow', 'pcol'))  481 us
    unnamed x4, waiting for transfers between devices  262 us
    all_gather x4, blocking collectives, per_device(): full_rows = lax.all_gather(own_piece, 'pcol', axis=1, tiled=True)  252 us
    psum x1, waiting for transfers between devices, broadcast(): return lax.psum(block, axis)  141 us
  transfers between devices with their start and end apart: 3, of which 3 were waited for; matrix products, arithmetic and copies ran while one was open for 1% of the time, Pallas kernels for 0%

commit v1 on v0

--- a/solution.py
+++ b/solution.py
@@ -72,7 +72,9 @@
         )
         keep_tiles = tile_flags.astype(jnp.bfloat16).reshape(tile_rows, 1, 1)
         own_piece = panels[later, :, 0] * keep_tiles
-        full_rows = lax.all_gather(own_piece, "pcol", axis=1, tiled=True)
+        full_rows = jnp.concatenate(
+            lax.all_to_all(jnp.stack([own_piece] * lax.axis_size("pcol")), "pcol", 0, 0), axis=1
+        )
         grouped = full_rows.reshape(owned_count, group_ratio, width, width)
         picked = lax.dynamic_slice_in_dim(grouped, column_index // prow_count, 1, 1)[:, 0]
         owned_tiles = broadcast(picked, "prow", column_index % prow_count)

time: 1210 us -> 1060 us (0.88)
  blocking collectives: 252 us -> 63.5 us
  waiting for transfers between devices: 884 us -> 922 us
    all_gather x4 -> x0, blocking collectives: 252 us -> none  [per_device(): full_rows = lax.all_gather(own_piece, 'pcol', axis=1, tiled=True)]
    all_to_all x0 -> x2, blocking collectives: none -> 63.5 us  [per_device(): lax.all_to_all(jnp.stack([own_piece] * lax.axis_size('pcol')), 'pcol', 0, 0)]
    all_to_all x0 -> x2, waiting for transfers between devices: none -> 38.5 us  [per_device(): lax.all_to_all(jnp.stack([own_piece] * lax.axis_size('pcol')), 'pcol', 0, 0)]
  transfers between devices with their start and end apart: 3 -> 5, of which waited for: 3 -> 5; matrix products, arithmetic and copies ran while one was open for 1% -> 1% of each run, Pallas kernels for 0% -> 0%
where the time goes in v1:
time: 1060 us
  waiting for transfers between devices  922 us (87%)
  blocking collectives  63.5 us (6%)
  local copies, waits for them, and re-layouts  20.8 us (2%)
  matrix products  19.6 us (2%)
  other arithmetic  15 us (1%)
  between operations  14.9 us (1%)
    psum x1, waiting for transfers between devices, per_device(): window_sums = lax.psum(jnp.stack(window_parts), ('prow', 'pcol'))  481 us
    unnamed x4, waiting for transfers between devices  262 us
    psum x1, waiting for transfers between devices, broadcast(): return lax.psum(block, axis)  141 us
    all_to_all x2, blocking collectives, per_device(): lax.all_to_all(jnp.stack([own_piece] * lax.axis_size('pcol')), 'pcol', 0, 0)  63.5 us
    all_to_all x2, waiting for transfers between devices, per_device(): lax.all_to_all(jnp.stack([own_piece] * lax.axis_size('pcol')), 'pcol', 0, 0)  38.5 us
  transfers between devices with their start and end apart: 5, of which 5 were waited for; matrix products, arithmetic and copies ran while one was open for 1% of the time, Pallas kernels for 0%

profile of v1, /device:TPU:4, one launch (start us, length us, event | category | flops | bytes accessed | tf_op | source)
XLA Modules:
  0.0 1063.5 jit_solution(8696860600660960613)
XLA Ops:
  7.2 0.8 slice_reduce_fusion.1
  8.8 0.8 bitcast_multiply_fusion.6
  9.7 38.5 %all_to_all.20 = bf16[32,2,8,256]{3,2,1,0:T(8,128)(2,1)S(1)} all-to-all(bf16[32,2,8,256]{3,2,1,0:T(8,128)(2,1)S(1)} %stack.45), channel_id=1, replica_groups=mesh['prow'=16,'pcol'=32] {'pcol'}, dimensions={0} | all-to-all | bytes 524288 | tf_op jit(solution)/shard_map/all_to_all | solution.py:76
  48.2 24.9 %all_to_all.21 = bf16[32,2,8,256]{3,2,1,0:T(8,128)(2,1)S(1)} all-to-all(bf16[32,2,8,256]{3,2,1,0:T(8,128)(2,1)S(1)} %stack.43), channel_id=1, replica_groups=mesh['prow'=16,'pcol'=32] {'pcol'}, dimensions={0} | all-to-all | bytes 524288 | tf_op jit(solution)/shard_map/all_to_all | solution.py:76
  73.9 3.9 all-to-all-start
  77.8 20.9 %all-to-all-done = bf16[32,2,8,256]{3,2,1,0:T(8,128)(2,1)S(1)} async-done(((bf16[32,2,8,256]{3,2,1,0:T(8,128)(2,1)}), bf16[32,2,8,256]{3,2,1,0:T(8,128)(2,1)S(1)}, u32[]{:S(2)}, u32[]{:S(2)}) %all-to-all-start) | async-done | bytes 262176 | tf_op jit(solution)/shard_map/all_to_all | solution.py:76
  99.4 3.9 all-to-all-start.3
  105.8 17.6 %all-to-all-done.3 = bf16[32,2,8,256]{3,2,1,0:T(8,128)(2,1)S(1)} async-done(((bf16[32,2,8,256]{3,2,1,0:T(8,128)(2,1)}), bf16[32,2,8,256]{3,2,1,0:T(8,128)(2,1)S(1)}, u32[]{:S(2)}, u32[]{:S(2)}) %all-to-all-start.3) | async-done | bytes 262176 | tf_op jit(solution)/shard_map/all_to_all | solution.py:76
  124.3 140.5 %all-reduce.15.cloned.1.call-done = (bf16[256,256]{0,1:T(8,128)(2,1)}, bf16[256,256]{0,1:T(8,128)(2,1)}, bf16[256,256]{0,1:T(8,128)(2,1)}, bf16[256,256]{0,1:T(8,128)(2,1)}) async-done(((bf16[256,256]{0,1:T(8,128)(2,1)}, bf16[256,256]{0,1:T(8,128)(2,1)}, bf16[256,256]{0,1:T(8,128)(2,1)}, bf16[256,256]{0,1:T(8,128)(2,1)}), (bf16[256,256]{0,1:T(8,128)(2,1)}, bf16[256,256]{0,1:T(8,128)(2,1)}, ...) | async-done | bytes 524304 | tf_op jit(solution)/shard_map/psum | solution.py:9
  264.8 1.2 convolution_bitcast_fusion
  266.0 1.0 copy.64
  267.3 1.0 copy.52
  268.5 1.0 copy.56
  269.8 1.0 copy.60
  274.5 5.0 broadcast_select_fusion
  279.5 1.3 dynamic-slice.15
  281.5 261.8 %all-reduce.13.cloned.1.call-done = (f32[256,2,256]{2,1,0:T(2,128)}, f32[256,2,256]{2,1,0:T(2,128)}, f32[256,2,256]{2,1,0:T(2,128)}, f32[256,2,256]{2,1,0:T(2,128)}) async-done(((f32[256,2,256]{2,1,0:T(2,128)}, f32[256,2,256]{2,1,0:T(2,128)}, f32[256,2,256]{2,1,0:T(2,128)}, f32[256,2,256]{2,1,0:T(2,128)}), (f32[256,2,256]{2,1,0:T(2,128)}, f32[256,2,256]{2,1,0:T(2,128)}, f32[256,2,256]{2,1,0:T(2,128)}, ...) | async-done | bytes 2097168
  545.2 1.1 convolution_bitcast_fusion.19
  552.7 0.9 pad_maximum_fusion.1
  553.6 1.1 pad_maximum_fusion
  555.4 480.8 %all-reduce.11.cloned.1.call-done = (f32[1,256,256]{2,1,0:T(8,128)}, f32[4,256,256]{2,1,0:T(8,128)}, f32[2,256,256]{2,1,0:T(8,128)}, f32[3,256,256]{2,1,0:T(8,128)}) async-done(((f32[1,256,256]{2,1,0:T(8,128)}, f32[4,256,256]{2,1,0:T(8,128)}, f32[2,256,256]{2,1,0:T(8,128)}, f32[3,256,256]{2,1,0:T(8,128)}), (f32[1,256,256]{2,1,0:T(8,128)}, f32[4,256,256]{2,1,0:T(8,128)}, f32[2,256,256]{2,1,0:T(8,128)}, ...) | async-done | bytes 2621456 | tf_op jit(solution)/shard_map/psum | solution.py:108
  1036.2 1.0 subtract_bitcast_fusion
  1037.3 1.3 fusion.14
  1041.0 1.0 fusion.7
  1042.4 0.8 copy.71
  1044.1 0.9 copy.75
  1044.9 0.9 copy.80
  1046.7 1.2 fusion.6
  1048.0 0.8 copy.74
  1048.8 2.0 fusion.3
  1053.2 1.9 fusion.1
  1055.2 1.1 maximum_maximum_fusion
  (114 shorter events, 26.5 us)
Async XLA Ops:
  7.2 257.6 %copy-start = (bf16[2,1,256,1,1,256]{5,2,4,3,1,0:T(8,128)(2,1)S(1)}, bf16[2,1,256,1,1,256]{5,2,4,3,1,0:T(8,128)(2,1)}, u32[]{:S(2)}) copy-start(bf16[2,1,256,1,1,256]{5,2,4,3,1,0:T(8,128)(2,1)} %param.15) | copy-start | bytes 786436
  73.9 24.9 %all-to-all-start = ((bf16[32,2,8,256]{3,2,1,0:T(8,128)(2,1)}), bf16[32,2,8,256]{3,2,1,0:T(8,128)(2,1)S(1)}, u32[]{:S(2)}, u32[]{:S(2)}) async-start(bf16[32,2,8,256]{3,2,1,0:T(8,128)(2,1)} %stack.42), calls=%async_computation | async-start | bytes 524288 | tf_op jit(solution)/shard_map/all_to_all | solution.py:76
  99.4 24.0 %all-to-all-start.3 = ((bf16[32,2,8,256]{3,2,1,0:T(8,128)(2,1)}), bf16[32,2,8,256]{3,2,1,0:T(8,128)(2,1)S(1)}, u32[]{:S(2)}, u32[]{:S(2)}) async-start(bf16[32,2,8,256]{3,2,1,0:T(8,128)(2,1)} %stack.47), calls=%async_computation.3 | async-start | bytes 524288 | tf_op jit(solution)/shard_map/all_to_all | solution.py:76
  103.3 161.5 %all-reduce.15.cloned.1.call-start = ((), (), s32[]{:S(2)}) async-start(), calls=%async_computation.6 | async-start | bytes 1048576 | tf_op jit(solution)/shard_map/psum | solution.py:9
  124.2 419.0 %all-reduce.13.cloned.1.call-start = ((), (), s32[]{:S(2)}) async-start(), calls=%async_computation.5 | async-start | bytes 4194304
  264.8 2.2 copy-start.11
  267.0 1.3 copy-start.10
  268.3 1.3 copy-start.9
  270.8 3.6 copy-start.12
  270.8 273.2 %copy-start.8 = (bf16[4,2,1,8,256]{4,3,2,1,0:T(8,128)(2,1)S(1)}, bf16[4,2,1,8,256]{4,3,2,1,0:T(8,128)(2,1)}, u32[]{:S(2)}) copy-start(bf16[4,2,1,8,256]{4,3,2,1,0:T(8,128)(2,1)} %param.16) | copy-start | bytes 98308
  270.9 276.8 %copy-start.1 = (bf16[6,256,256]{2,1,0:T(8,128)(2,1)S(1)}, bf16[6,256,256]{2,1,0:T(8,128)(2,1)}, u32[]{:S(2)}) copy-start(bf16[6,256,256]{2,1,0:T(8,128)(2,1)} %param.18) | copy-start | bytes 2359300
  270.9 765.3 %all-reduce.11.cloned.1.call-start = ((), (), s32[]{:S(2)}) async-start(), calls=%async_computation.4 | async-start | bytes 5242880 | tf_op jit(solution)/shard_map/psum | solution.py:108
  554.7 481.5 %copy-start.7 = (bf16[4,256,256]{2,1,0:T(8,128)(2,1)S(1)}, bf16[4,256,256]{2,1,0:T(8,128)(2,1)}, u32[]{:S(2)}) copy-start(bf16[4,256,256]{2,1,0:T(8,128)(2,1)} %param.19) | copy-start | bytes 1572868
  1036.2 2.4 copy-start.6
  1037.3 1.7 copy-start.2
  1038.9 1.1 copy-start.5
  1045.8 0.9 copy-start.4
  1051.6 0.9 copy-start.3
Sparse Core Ops, SparseCore 0:
  124.4 140.3 all-reduce.14
  271.0 272.2 all-reduce.12
  554.8 481.3 all-reduce.10
